TPU v7x, 32 devices: a whole 2x2x4 slice. The times are simulated.
32 devices in a mesh: dp: 2 (over x), expert: 16 (over z, y, core).
Axes of the slice: x: 2, y: 2, z: 4, core: 2. Of those that a mesh axis runs over, the one named last changes fastest.
Arguments:
- tokens: bfloat16 [4096, 2048], P(('dp', 'expert')), may hold values from -6 to 6
- gate_weights: float32 [4096, 2], P(('dp', 'expert')), may hold values from 0.02 to 0.5
- expert_ids: int32 [4096, 2], P(('dp', 'expert')), may hold values from 0 to 15, as said below
- hot_experts: int32 [4], replicated, may hold values from 0 to 15, as said below
- gate_proj: bfloat16 [16, 2048, 768], P('expert', 'dp'), may hold values from -0.125 to 0.125
- up_proj: bfloat16 [16, 2048, 768], P('expert', 'dp'), may hold values from -0.125 to 0.125
- down_proj: bfloat16 [16, 2048, 768], P('expert', 'dp'), may hold values from -0.21875 to 0.21875
- out_grad: bfloat16 [4096, 2048], P(('dp', 'expert')), may hold values from -6 to 6
Outputs:
- layer_out: bfloat16 [4096, 2048], P(('dp', 'expert'))
- tokens_grad: bfloat16 [4096, 2048], P(('dp', 'expert'))
- routing_grad: float32 [4096, 2], P(('dp', 'expert'))
- gate_proj_grad: bfloat16 [16, 2048, 768], P('expert', 'dp')
- up_proj_grad: bfloat16 [16, 2048, 768], P('expert', 'dp')
- down_proj_grad: bfloat16 [16, 2048, 768], P('expert', 'dp')
Inputs may be any that keep to these rules, and one draw needn't show every extreme that they name: `expert_ids`: each token names 2 different experts. In each block of 128 rows of one device no expert is named more than 28 times, and the expert hot_experts[0] is named exactly 28 times in every block. `hot_experts`: 4 different experts.
All inputs are finite; a program needn't handle non-finite values.
Results may differ from a plain program's by a relative error of at most 0.012.
Values may be sent and summed in bfloat16 or wider, within the bound.
No kernel may reach another device: no remote copies, remote signals or barrier semaphores. Data moves between devices by JAX's collectives and lax.ppermute only.
A program may use at most 128 MiB of HBM per device.

v0:
```python
import jax
import jax.numpy as jnp
from jax import lax
from jax.sharding import PartitionSpec as P

TOPK = 2


def contract_last(left_side, right_side):
    return lax.dot_general(
        left_side, right_side, (((1,), (1,)), ((), ())), preferred_element_type=jnp.float32
    )


def contract_first(left_side, right_side):
    return lax.dot_general(
        left_side, right_side, (((0,), (0,)), ((), ())), preferred_element_type=jnp.float32
    )


def body(tokens, gate_weights, expert_ids, hot_experts, gate_proj, up_proj, down_proj, out_grad):
    owners = lax.axis_size("expert")
    model_width = tokens.shape[1]
    token_count = tokens.shape[0]
    assign_count = token_count * TOPK
    cap_rows = 5 * assign_count // (4 * owners)
    slot_count = cap_rows + assign_count // (2 * owners)
    local_gate = gate_proj[0]
    local_up = up_proj[0]
    local_down = down_proj[0]
    hidden_units = local_gate.shape[1]
    flat_ids = expert_ids.reshape(-1)
    expert_range = jnp.arange(owners, dtype=jnp.int32)
    onehot = (flat_ids[:, None] == expert_range[None, :]).astype(jnp.int32)
    before = jnp.cumsum(onehot, axis=0) - onehot
    slot_pos = jnp.sum(before * onehot, axis=1)
    hot_flags = jnp.sum((hot_experts[:, None] == expert_range[None, :]).astype(jnp.int32), axis=0)
    hot_row = jnp.sum(onehot * hot_flags[None, :], axis=1) > 0
    kept_mask = slot_pos < jnp.where(hot_row, slot_count, cap_rows)
    row_slot = flat_ids * slot_count + jnp.minimum(slot_pos, slot_count - 1)
    target = jnp.where(kept_mask, row_slot, -1)
    placing = (jnp.arange(owners * slot_count, dtype=jnp.int32)[:, None] == target[None, :]).astype(
        jnp.bfloat16
    )
    token_place = placing.reshape(owners * slot_count, token_count, TOPK).sum(axis=2)
    send_rows = jnp.dot(token_place, tokens, preferred_element_type=jnp.float32).astype(
        jnp.bfloat16
    )
    send_rows = send_rows.reshape(owners, slot_count, model_width)
    received = lax.all_to_all(send_rows, "expert", split_axis=0, concat_axis=0, tiled=True)
    expert_expert_rows = received.reshape(-1, model_width)
    pieces = (
        lax.all_gather(local_gate, "dp", axis=0, tiled=True),
        lax.all_gather(local_up, "dp", axis=0, tiled=True),
    )
    columns = expert_expert_rows
    gate_act = jnp.dot(columns, pieces[0], preferred_element_type=jnp.float32)
    up_act = jnp.dot(columns, pieces[1], preferred_element_type=jnp.float32)
    expert_hidden = (gate_act * jax.nn.sigmoid(gate_act) * up_act).astype(jnp.bfloat16)
    output = contract_last(
        expert_hidden, lax.all_gather(local_down, "dp", axis=0, tiled=True)
    ).astype(jnp.bfloat16)
    returned = lax.all_to_all(
        output.reshape(received.shape), "expert", split_axis=0, concat_axis=0, tiled=True
    )
    act_shape = (received.shape[0], received.shape[1], hidden_units)
    returned, saved_rows, saved_gate, saved_up = (
        returned,
        received,
        gate_act.reshape(act_shape),
        up_act.reshape(act_shape),
    )
    safe_slot = jnp.where(kept_mask, row_slot, 0)
    keep_scale = kept_mask.astype(jnp.float32)[:, None]
    chosen = (
        jnp.take(returned.reshape(-1, model_width), safe_slot, axis=0).astype(jnp.float32)
        * keep_scale
    )
    weight_flat = gate_weights.reshape(-1, 1)
    layer_out = (
        (chosen * weight_flat)
        .reshape(token_count, TOPK, model_width)
        .sum(axis=1)
        .astype(jnp.bfloat16)
    )
    routing_grad = jnp.sum(
        chosen.reshape(token_count, TOPK, model_width) * out_grad.astype(jnp.float32)[:, None, :],
        axis=2,
    )
    spread = (weight_flat * jnp.repeat(out_grad, TOPK, axis=0).astype(jnp.float32)).astype(
        jnp.bfloat16
    )
    grad_send = jnp.dot(placing, spread, preferred_element_type=jnp.float32).astype(jnp.bfloat16)
    grad_recv = lax.all_to_all(
        grad_send.reshape(owners, slot_count, model_width),
        "expert",
        split_axis=0,
        concat_axis=0,
        tiled=True,
    )
    grad_in = grad_recv.reshape(-1, model_width)
    expert_rows = saved_rows.reshape(-1, model_width)
    gate_act = saved_gate.reshape(-1, hidden_units)
    up_act = saved_up.reshape(-1, hidden_units)
    columns = grad_in
    grad_hidden = jnp.dot(
        columns,
        lax.all_gather(local_down, "dp", axis=0, tiled=True),
        preferred_element_type=jnp.float32,
    )
    sigmoid_act = jax.nn.sigmoid(gate_act)
    silu_act = gate_act * sigmoid_act
    hidden = (silu_act * up_act).astype(jnp.bfloat16)
    grad_up = (grad_hidden * silu_act).astype(jnp.bfloat16)
    grad_gate = (
        grad_hidden * up_act * sigmoid_act * (1.0 + gate_act * (1.0 - sigmoid_act))
    ).astype(jnp.bfloat16)
    pieces = lax.all_gather((local_gate, local_up), "dp", axis=0, tiled=True)
    grad_rows = (contract_last(grad_gate, pieces[0]) + contract_last(grad_up, pieces[1])).astype(
        jnp.bfloat16
    )
    grad_back = lax.all_to_all(
        grad_rows.reshape(owners, slot_count, model_width),
        "expert",
        split_axis=0,
        concat_axis=0,
        tiled=True,
    )
    chosen_grad = (
        jnp.take(grad_back.reshape(-1, model_width), safe_slot, axis=0).astype(jnp.float32)
        * keep_scale
    )
    tokens_grad = (
        chosen_grad.reshape(token_count, TOPK, model_width).sum(axis=1).astype(jnp.bfloat16)
    )
    summed = lax.psum_scatter(
        jnp.concatenate(
            [
                contract_first(expert_rows, grad_gate),
                contract_first(expert_rows, grad_up),
                contract_first(grad_in, hidden),
            ],
            axis=1,
        ).astype(jnp.bfloat16),
        "dp",
        scatter_dimension=0,
        tiled=True,
    ).astype(jnp.float32)
    gate_proj_grad = summed[:, :hidden_units].astype(jnp.bfloat16)[None]
    up_proj_grad = summed[:, hidden_units : 2 * hidden_units].astype(jnp.bfloat16)[None]
    down_proj_grad = summed[:, 2 * hidden_units :].astype(jnp.bfloat16)[None]
    return (layer_out, tokens_grad, routing_grad, gate_proj_grad, up_proj_grad, down_proj_grad)


def solution(mesh):
    in_specs = (
        P(("dp", "expert"), None),
        P(("dp", "expert"), None),
        P(("dp", "expert"), None),
        P(),
        P("expert", "dp", None),
        P("expert", "dp", None),
        P("expert", "dp", None),
        P(("dp", "expert"), None),
    )
    out_specs = (
        P(("dp", "expert"), None),
        P(("dp", "expert"), None),
        P(("dp", "expert"), None),
        P("expert", "dp", None),
        P("expert", "dp", None),
        P("expert", "dp", None),
    )
    return jax.shard_map(body, mesh=mesh, in_specs=in_specs, out_specs=out_specs, check_vma=False)
```

profile of v0, /device:TPU:13, one launch (start us, length us, event | category | flops | bytes accessed | tf_op | source)
XLA Modules:
  0.0 318.9 jit_solution(3125575328886771847)
XLA Ops:
  9.0 2.4 broadcast_in_dim.51
  11.4 2.7 convert_element_type.84
  17.4 3.7 %reshape.124 = bf16[16,28,2048]{2,1,0:T(8,128)(2,1)} reshape(bf16[448,2048]{1,0:T(8,128)(2,1)} %convolution_convert_fusion.3) | data formatting | bytes 3670016 | tf_op jit(solution)/shard_map/reshape | solution.py:95
  21.1 6.7 %all-to-all-start.2 = ((bf16[16,28,2048]{2,1,0:T(8,128)(2,1)}), bf16[16,28,2048]{2,1,0:T(8,128)(2,1)S(1)}, u32[]{:S(2)}, u32[]{:S(2)}) async-start(bf16[16,28,2048]{2,1,0:T(8,128)(2,1)} %reshape.124), calls=%async_computation.2 | async-start | bytes 4194304 | tf_op jit(solution)/shard_map/all_to_all | solution.py:94
  31.0 3.5 %reshape.119 = bf16[16,28,2048]{2,1,0:T(8,128)(2,1)} reshape(bf16[448,2048]{1,0:T(8,128)(2,1)} %convolution_convert_fusion.4) | data formatting | bytes 3670016 | tf_op jit(solution)/shard_map/reshape | solution.py:49
  34.5 41.1 %all-to-all-done.2 = bf16[16,28,2048]{2,1,0:T(8,128)(2,1)S(1)} async-done(((bf16[16,28,2048]{2,1,0:T(8,128)(2,1)}), bf16[16,28,2048]{2,1,0:T(8,128)(2,1)S(1)}, u32[]{:S(2)}, u32[]{:S(2)}) %all-to-all-start.2) | async-done | bytes 1835040 | tf_op jit(solution)/shard_map/all_to_all | solution.py:94
  75.6 4.4 %all-to-all-start = ((bf16[16,28,2048]{2,1,0:T(8,128)(2,1)}), bf16[16,28,2048]{2,1,0:T(8,128)(2,1)}, u32[]{:S(2)}, u32[]{:S(2)}) async-start(bf16[16,28,2048]{2,1,0:T(8,128)(2,1)} %reshape.119), calls=%async_computation | async-start | bytes 4194304 | tf_op jit(solution)/shard_map/all_to_all | solution.py:50
  82.4 45.4 %all-to-all-done = bf16[16,28,2048]{2,1,0:T(8,128)(2,1)} async-done(((bf16[16,28,2048]{2,1,0:T(8,128)(2,1)}), bf16[16,28,2048]{2,1,0:T(8,128)(2,1)}, u32[]{:S(2)}, u32[]{:S(2)}) %all-to-all-start) | async-done | bytes 1835040 | tf_op jit(solution)/shard_map/all_to_all | solution.py:50
  127.8 3.6 %reshape.120 = bf16[448,2048]{1,0:T(8,128)(2,1)} reshape(bf16[16,28,2048]{2,1,0:T(8,128)(2,1)} %all-to-all-done) | data formatting | bytes 3670016 | tf_op jit(solution)/shard_map/reshape | solution.py:51
  131.4 4.6 %fusion = f32[448,768]{1,0:T(8,128)} fusion(bf16[448,2048]{1,0:T(8,128)(2,1)S(1)} %copy-done.5, bf16[1,2048,768]{2,1,0:T(8,128)(2,1)} %all-gather.11.cloned.1.call-done), kind=kOutput, calls=%fused_computation.7 | convolution fusion | flops 1409286144 | bytes 6356992 | tf_op jit(solution)/shard_map/dot_general | solution.py:106
  136.0 5.1 %fusion.6 = f32[448,768]{1,0:T(8,128)} fusion(bf16[448,2048]{1,0:T(8,128)(2,1)} %reshape.120, bf16[1,2048,768]{2,1,0:T(8,128)(2,1)} %all-gather.9.cloned.1.call-done), kind=kOutput, calls=%fused_computation.13 | convolution fusion | flops 1409286144 | bytes 6356992 | tf_op jit(solution)/shard_map/dot_general | solution.py:58
  141.1 7.4 %all-gather.7.cloned.1.call-done = bf16[1,2048,768]{2,1,0:T(8,128)(2,1)} async-done(((bf16[1,1024,768]{2,1,0:T(8,128)(2,1)}), bf16[1,2048,768]{2,1,0:T(8,128)(2,1)}) %all-gather.7.cloned.1.call-update) | async-done | bytes 3145744 | tf_op jit(solution)/shard_map/all_gather | solution.py:53
  148.4 5.3 %multiply_convert_fusion.2 = (bf16[448,768]{1,0:T(8,128)(2,1)S(1)}, bf16[448,768]{1,0:T(8,128)(2,1)S(1)}, bf16[448,768]{1,0:T(8,128)(2,1)S(1)}) fusion(f32[448,768]{1,0:T(8,128)} %fusion, f32[448,768]{1,0:T(8,128)} %fusion.6, bf16[448,2048]{1,0:T(8,128)(2,1)} %reshape.120, bf16[1,2048,768]{2,1,0:T(8,128)(2,1)} %all-gather.7.cloned.1.call-done), kind=kOutput, calls=%fused_computation.31 | convolution fusion | flops 1414447104 | bytes 9797632 | tf_op jit(solution)/shard_map/dot_general | solution.py:57
  159.5 4.5 %pad_maximum_fusion = bf16[2048,2304]{0,1:T(8,128)(2,1)} fusion(bf16[2048,768]{0,1:T(8,128)(2,1)S(1)} %convolution_convert_fusion, bf16[2048,768]{0,1:T(8,128)(2,1)S(1)} %convolution_convert_fusion.1, bf16[2048,768]{0,1:T(8,128)(2,1)S(1)} %convolution_convert_fusion.2), kind=kLoop, calls=%fused_computation.2 | loop fusion | flops 28311552 | bytes 18874368 | tf_op jit(solution)/shard_map/concatenate | solution.py:137
  164.0 3.7 %fusion.12 = bf16[448,2048]{1,0:T(8,128)(2,1)S(1)} fusion(bf16[448,768]{1,0:T(8,128)(2,1)} %copy-done.12, bf16[1,2048,768]{2,1,0:T(8,128)(2,1)} %all-gather.11.cloned.1.call-done), kind=kOutput, calls=%fused_computation.21 | convolution fusion | flops 1410203648 | bytes 5668864 | tf_op jit(solution)/shard_map/dot_general | solution.py:10
  169.3 6.5 %all-to-all-start.1 = ((bf16[16,28,2048]{2,1,0:T(8,128)(2,1)}), bf16[16,28,2048]{2,1,0:T(8,128)(2,1)S(1)}, u32[]{:S(2)}, u32[]{:S(2)}) async-start(bf16[16,28,2048]{2,1,0:T(8,128)(2,1)} %reshape.121), calls=%async_computation.1 | async-start | bytes 4194304 | tf_op jit(solution)/shard_map/all_to_all | solution.py:63
  175.8 3.7 %fusion.4 = f32[448,2048]{1,0:T(8,128)S(1)} fusion(bf16[448,768]{1,0:T(8,128)(2,1)S(1)} %get-tuple-element.41, bf16[1,2048,768]{2,1,0:T(8,128)(2,1)} %all-gather.9.cloned.1.call-done), kind=kOutput, calls=%fused_computation.11 | convolution fusion | flops 1409286144 | bytes 7503872 | tf_op jit(solution)/shard_map/dot_general | solution.py:10
  179.5 2.9 add_convert_fusion
  182.3 3.5 %reshape.126 = bf16[16,28,2048]{2,1,0:T(8,128)(2,1)} reshape(bf16[448,2048]{1,0:T(8,128)(2,1)} %add_convert_fusion) | data formatting | bytes 3670016 | tf_op jit(solution)/shard_map/reshape | solution.py:123
  185.9 37.7 %all-to-all-done.1 = bf16[16,28,2048]{2,1,0:T(8,128)(2,1)S(1)} async-done(((bf16[16,28,2048]{2,1,0:T(8,128)(2,1)}), bf16[16,28,2048]{2,1,0:T(8,128)(2,1)S(1)}, u32[]{:S(2)}, u32[]{:S(2)}) %all-to-all-start.1) | async-done | bytes 1835040 | tf_op jit(solution)/shard_map/all_to_all | solution.py:63
  224.9 4.6 %all-to-all-start.3 = ((bf16[16,28,2048]{2,1,0:T(8,128)(2,1)}), bf16[16,28,2048]{2,1,0:T(8,128)(2,1)}, u32[]{:S(2)}, u32[]{:S(2)}) async-start(bf16[16,28,2048]{2,1,0:T(8,128)(2,1)} %reshape.126), calls=%async_computation.3 | async-start | bytes 4194304 | tf_op jit(solution)/shard_map/all_to_all | solution.py:122
  229.5 2.6 reshape.122
  232.1 2.3 gather_fusion
  234.4 42.4 %all-to-all-done.3 = bf16[16,28,2048]{2,1,0:T(8,128)(2,1)} async-done(((bf16[16,28,2048]{2,1,0:T(8,128)(2,1)}), bf16[16,28,2048]{2,1,0:T(8,128)(2,1)}, u32[]{:S(2)}, u32[]{:S(2)}) %all-to-all-start.3) | async-done | bytes 1835040 | tf_op jit(solution)/shard_map/all_to_all | solution.py:122
  276.8 2.5 reshape.127
  281.6 4.2 %multiply_reduce_fusion = (f32[256]{0:T(256)S(1)}, f32[256,2048]{1,0:T(8,128)}, f32[256,2048]{1,0:T(8,128)S(1)}) fusion(f32[256,2048]{1,0:T(8,128)} %copy-done.2, f32[256]{0:T(256)S(1)} %get-tuple-element.47, bf16[256,2048]{1,0:T(8,128)(2,1)} %gather_fusion, pred[256]{0:T(512)(128)(4,1)S(1)} %get-tuple-element.35, f32[256]{0:T(256)S(1)} %mul.91, ...), kind=kLoop, calls=%fused_computation.22 | loop fusion | flops 4718336 | bytes 8391936 | tf_op jit(solution)/shard_map/reduce_sum | solution.py:86
  285.8 3.4 %reshape.123 = f32[128,2,2048]{2,1,0:T(2,128)} reshape(f32[256,2048]{1,0:T(8,128)} %get-tuple-element.44) | data formatting | bytes 4194304 | tf_op jit(solution)/shard_map/reshape | solution.py:82
  291.4 5.1 %reduce_sum.72 = bf16[128,2048]{1,0:T(8,128)(2,1)} reduce(f32[128,2,2048]{2,1,0:T(2,128)} %reshape.123, f32[]{:T(128)} %constant.32.clone.1), dimensions={1}, to_apply=%region_6.8 | reduce | flops 262144 | bytes 2621444 | tf_op jit(solution)/shard_map/reduce_sum | solution.py:83
  296.5 3.8 %reduce_sum.73 = bf16[128,2048]{1,0:T(8,128)(2,1)} reduce(f32[128,2,2048]{2,1,0:T(2,128)S(1)} %copy-done.4, f32[]{:T(128)} %constant.32.clone.1), dimensions={1}, to_apply=%region_7.9 | reduce | flops 262144 | bytes 2621444 | tf_op jit(solution)/shard_map/reduce_sum | solution.py:134
  301.1 4.5 %slice_bitcast_fusion = (bf16[1,1024,768]{1,2,0:T(8,128)(2,1)S(1)}, bf16[1,1024,768]{1,2,0:T(8,128)(2,1)}, bf16[1,1024,768]{1,2,0:T(8,128)(2,1)}) fusion(bf16[1024,2304]{0,1:T(8,128)(2,1)} %reduce-scatter.2.cloned.1.call-done), kind=kLoop, calls=%fused_computation.27 | loop fusion | bytes 9437184 | tf_op jit(solution)/shard_map/broadcast_in_dim | solution.py:151
  305.6 2.6 copy.46
  308.2 2.6 copy.47
  (74 shorter events, 26.1 us)
Async XLA Ops:
  7.2 21.9 %copy-start = (bf16[128,2048]{1,0:T(8,128)(2,1)S(1)}, bf16[128,2048]{1,0:T(8,128)(2,1)}, u32[]{:S(2)}) copy-start(bf16[128,2048]{1,0:T(8,128)(2,1)} %param.10) | copy-start | bytes 1572868
  7.2 1.8 copy-start.7
  7.2 124.2 %all-gather.11.cloned.1.call-start = ((), (), s32[]{:S(2)}) async-start(), calls=%async_computation.8 | async-start | bytes 4718592 | tf_op jit(solution)/shard_map/all_gather | solution.py:61
  11.4 3.6 %copy-start.9 = (f32[128,2]{0,1:T(2,128)S(1)}, f32[128,2]{0,1:T(2,128)}, u32[]{:S(2)}) copy-start(f32[128,2]{0,1:T(2,128)} %param.11) | copy-start | bytes 3076
  11.4 3.8 %copy-start.11 = (s32[4]{0:T(128)S(1)}, s32[4]{0:T(128)}, u32[]{:S(2)}) copy-start(s32[4]{0:T(128)} %param.13) | copy-start | bytes 52
  14.1 7.0 %copy-start.2 = (f32[256,2048]{1,0:T(8,128)}, f32[256,2048]{1,0:T(8,128)S(1)}, u32[]{:S(2)}) copy-start(f32[256,2048]{1,0:T(8,128)S(1)} %convert_element_type.84) | copy-start | bytes 6291460
  21.1 7.9 %copy-start.8 = (s32[128,2]{0,1:T(2,128)S(1)}, s32[128,2]{0,1:T(2,128)}, u32[]{:S(2)}) copy-start(s32[128,2]{0,1:T(2,128)} %param.12) | copy-start | bytes 3076
  21.1 54.5 %all-to-all-start.2 = ((bf16[16,28,2048]{2,1,0:T(8,128)(2,1)}), bf16[16,28,2048]{2,1,0:T(8,128)(2,1)S(1)}, u32[]{:S(2)}, u32[]{:S(2)}) async-start(bf16[16,28,2048]{2,1,0:T(8,128)(2,1)} %reshape.124), calls=%async_computation.2 | async-start | bytes 4194304 | tf_op jit(solution)/shard_map/all_to_all | solution.py:94
  27.8 108.2 %all-gather.9.cloned.1.call-start = ((), (), s32[]{:S(2)}) async-start(), calls=%async_computation.7 | async-start | bytes 4718592 | tf_op jit(solution)/shard_map/all_gather | solution.py:54
  75.6 52.2 %all-to-all-start = ((bf16[16,28,2048]{2,1,0:T(8,128)(2,1)}), bf16[16,28,2048]{2,1,0:T(8,128)(2,1)}, u32[]{:S(2)}, u32[]{:S(2)}) async-start(bf16[16,28,2048]{2,1,0:T(8,128)(2,1)} %reshape.119), calls=%async_computation | async-start | bytes 4194304 | tf_op jit(solution)/shard_map/all_to_all | solution.py:50
  80.0 68.4 %all-gather.7.cloned.1.call-start = ((), (), s32[]{:S(2)}) async-start(), calls=%async_computation.6 | async-start | bytes 4718592 | tf_op jit(solution)/shard_map/all_gather | solution.py:53
  80.7 220.4 %reduce-scatter.2.cloned.1.call-start = ((), (), s32[]{:S(2)}) async-start(), calls=%async_computation.5 | async-start | bytes 14155776 | tf_op jit(solution)/shard_map/reduce_scatter | solution.py:136
  82.4 49.0 %copy-start.5 = (bf16[448,2048]{1,0:T(8,128)(2,1)S(1)}, bf16[448,2048]{1,0:T(8,128)(2,1)}, u32[]{:S(2)}) copy-start(bf16[448,2048]{1,0:T(8,128)(2,1)} %reshape.125) | copy-start | bytes 5505028
  153.7 1.9 copy-start.12
  153.7 3.9 %copy-start.13 = (bf16[448,768]{1,0:T(8,128)(2,1)}, bf16[448,768]{1,0:T(8,128)(2,1)S(1)}, u32[]{:S(2)}) copy-start(bf16[448,768]{1,0:T(8,128)(2,1)S(1)} %get-tuple-element.40) | copy-start | bytes 2064388
  153.7 2.0 copy-start.6
  169.3 54.3 %all-to-all-start.1 = ((bf16[16,28,2048]{2,1,0:T(8,128)(2,1)}), bf16[16,28,2048]{2,1,0:T(8,128)(2,1)S(1)}, u32[]{:S(2)}, u32[]{:S(2)}) async-start(bf16[16,28,2048]{2,1,0:T(8,128)(2,1)} %reshape.121), calls=%async_computation.1 | async-start | bytes 4194304 | tf_op jit(solution)/shard_map/all_to_all | solution.py:63
  175.8 3.7 %copy-start.10 = (bf16[1,2048,768]{2,1,0:T(8,128)(2,1)S(1)}, bf16[1,2048,768]{2,1,0:T(8,128)(2,1)}, u32[]{:S(2)}) copy-start(bf16[1,2048,768]{2,1,0:T(8,128)(2,1)} %all-gather.7.cloned.1.call-done) | copy-start | bytes 9437188
  175.8 3.7 %copy-start.14 = (bf16[448,768]{1,0:T(8,128)(2,1)S(1)}, bf16[448,768]{1,0:T(8,128)(2,1)}, u32[]{:S(2)}) copy-start(bf16[448,768]{1,0:T(8,128)(2,1)} %copy-done.13) | copy-start | bytes 2064388
  223.6 1.3 copy-start.3
  224.9 51.9 %all-to-all-start.3 = ((bf16[16,28,2048]{2,1,0:T(8,128)(2,1)}), bf16[16,28,2048]{2,1,0:T(8,128)(2,1)}, u32[]{:S(2)}, u32[]{:S(2)}) async-start(bf16[16,28,2048]{2,1,0:T(8,128)(2,1)} %reshape.126), calls=%async_computation.3 | async-start | bytes 4194304 | tf_op jit(solution)/shard_map/all_to_all | solution.py:122
  291.4 5.1 %copy-start.4 = (f32[128,2,2048]{2,1,0:T(2,128)S(1)}, f32[128,2,2048]{2,1,0:T(2,128)}, u32[]{:S(2)}) copy-start(f32[128,2,2048]{2,1,0:T(2,128)} %reshape.128) | copy-start | bytes 6291460
  308.2 4.2 %copy-start.1 = (bf16[128,2048]{1,0:T(8,128)(2,1)S(1)}, bf16[128,2048]{1,0:T(8,128)(2,1)}, u32[]{:S(2)}) copy-start(bf16[128,2048]{1,0:T(8,128)(2,1)} %param.10) | copy-start | bytes 1572868
Sparse Core Ops, SparseCore 0:
  9.5 45.8 all-gather.10
  57.0 44.8 all-gather.8
  103.5 44.8 all-gather.6
  164.1 110.6 reduce-scatter.1
where the time goes:
time: 320 us; the launch traced here: 319 us
  waiting for transfers between devices  176 us (55%)
  local copies, waits for them, and re-layouts  53.2 us (17%)
  matrix products  34.7 us (11%)
  starting transfers between devices  22.4 us (7%)
  other arithmetic  18.4 us (6%)
  between operations  14 us (4%)
    all_to_all x1, waiting for transfers between devices, body(): lax.all_to_all(send_rows, 'expert', split_axis=0, concat_axis=0, tiled=True)  45.4 us
    all_to_all x1, waiting for transfers between devices, body(): lax.all_to_all(grad_rows.reshape(owners, slot_count, model_width), 'exper...  42.4 us
    all_to_all x1, waiting for transfers between devices, body(): lax.all_to_all(grad_send.reshape(owners, slot_count, model_width), 'exper...  41.1 us
    all_to_all x1, waiting for transfers between devices, body(): lax.all_to_all(output.reshape(received.shape), 'expert', split_axis=0, co...  37.7 us
    dot_general x3, matrix products, contract_last(): lax.dot_general(left_side, right_side, (((1,), (1,)), ((), ())), preferre...  10.3 us
    unnamed x36, local copies, waits for them, and re-layouts  9.8 us
    all_gather x1, waiting for transfers between devices, body(): lax.all_gather(local_gate, 'dp', axis=0, tiled=True)  7.35 us
    all_to_all x1, starting transfers between devices, body(): lax.all_to_all(grad_send.reshape(owners, slot_count, model_width), 'exper...  6.66 us
  transfers between devices with their start and end apart: 8, of which 5 were waited for; matrix products, arithmetic and copies ran while one was open for 25% of the time, Pallas kernels for 0%

commit v1 on v0

--- a/solution.py
+++ b/solution.py
@@ -4,6 +4,22 @@
 from jax.sharding import PartitionSpec as P
 
 TOPK = 2
+
+
+def pairwise_exchange(shard, axis, split, join):
+    ways, here = (lax.axis_size(axis), lax.axis_index(axis))
+    width = shard.shape[split] // ways
+    dims = list(shard.shape)
+    dims[split] = width
+    height = dims[join]
+    dims[join] = height * ways
+    full = jnp.zeros(dims, shard.dtype)
+    for mask in range(ways):
+        part = lax.dynamic_slice_in_dim(shard, (here ^ mask) * width, width, axis=split)
+        if mask:
+            part = lax.ppermute(part, axis, [(d, d ^ mask) for d in range(ways)])
+        full = lax.dynamic_update_slice_in_dim(full, part, (here ^ mask) * height, axis=join)
+    return full
 
 
 def contract_last(left_side, right_side):
@@ -119,12 +135,8 @@
     grad_rows = (contract_last(grad_gate, pieces[0]) + contract_last(grad_up, pieces[1])).astype(
         jnp.bfloat16
     )
-    grad_back = lax.all_to_all(
-        grad_rows.reshape(owners, slot_count, model_width),
-        "expert",
-        split_axis=0,
-        concat_axis=0,
-        tiled=True,
+    grad_back = pairwise_exchange(
+        grad_rows.reshape(owners, slot_count, model_width), "expert", 0, 0
     )
     chosen_grad = (
         jnp.take(grad_back.reshape(-1, model_width), safe_slot, axis=0).astype(jnp.float32)

time: 320 us -> 330 us (1.031)
  starting transfers between devices: 22.4 us -> 42.7 us
  waiting for transfers between devices: 176 us -> 156 us
  local copies, waits for them, and re-layouts: 53.2 us -> 63.9 us
    ppermute x0 -> x15, waiting for transfers between devices: none -> 60 us  [pairwise_exchange(): part = lax.ppermute(part, axis, [(d, d ^ mask) for d in range(ways)])]
    all_to_all x1 -> x0, waiting for transfers between devices: 42.4 us -> none  [body(): lax.all_to_all(grad_rows.reshape(owners, slot_count, model_width), 'exper...]
    all_to_all x1, waiting for transfers between devices: 37.7 us -> 0.01 us  [body(): lax.all_to_all(output.reshape(received.shape), 'expert', split_axis=0, co...]
    ppermute x0 -> x15, starting transfers between devices: none -> 24.8 us  [pairwise_exchange(): part = lax.ppermute(part, axis, [(d, d ^ mask) for d in range(ways)])]
    dynamic_update_slice x0 -> x15, local copies, waits for them, and re-layouts: none -> 9.85 us  [pairwise_exchange(): lax.dynamic_update_slice_in_dim(full, part, (here ^ mask) * height, axis=...]
    all_to_all x1 -> x0, starting transfers between devices: 4.56 us -> none  [body(): lax.all_to_all(grad_rows.reshape(owners, slot_count, model_width), 'exper...]
    unnamed x36 -> x46, local copies, waits for them, and re-layouts: 9.8 us -> 9.11 us
  transfers between devices with their start and end apart: 8 -> 22, of which waited for: 5 -> 14; matrix products, arithmetic and copies ran while one was open for 25% -> 27% of each run, Pallas kernels for 0% -> 0%
where the time goes in v1:
time: 330 us; the launch traced here: 328 us
  waiting for transfers between devices  156 us (47%)
  local copies, waits for them, and re-layouts  63.9 us (19%)
  starting transfers between devices  42.7 us (13%)
  matrix products  32.6 us (10%)
  other arithmetic  18.9 us (6%)
  between operations  14.2 us (4%)
    ppermute x15, waiting for transfers between devices, pairwise_exchange(): part = lax.ppermute(part, axis, [(d, d ^ mask) for d in range(ways)])  60 us
    all_to_all x1, waiting for transfers between devices, body(): lax.all_to_all(send_rows, 'expert', split_axis=0, concat_axis=0, tiled=True)  45.4 us
    all_to_all x1, waiting for transfers between devices, body(): lax.all_to_all(grad_send.reshape(owners, slot_count, model_width), 'exper...  41.1 us
    ppermute x15, starting transfers between devices, pairwise_exchange(): part = lax.ppermute(part, axis, [(d, d ^ mask) for d in range(ways)])  24.8 us
    dynamic_update_slice x15, local copies, waits for them, and re-layouts, pairwise_exchange(): lax.dynamic_update_slice_in_dim(full, part, (here ^ mask) * height, axis=...  9.85 us
    unnamed x46, local copies, waits for them, and re-layouts  9.11 us
    dot_general x3, matrix products, contract_last(): lax.dot_general(left_side, right_side, (((1,), (1,)), ((), ())), preferre...  8.18 us
    all_gather x1, waiting for transfers between devices, body(): lax.all_gather(local_gate, 'dp', axis=0, tiled=True)  7.35 us
  transfers between devices with their start and end apart: 22, of which 14 were waited for; matrix products, arithmetic and copies ran while one was open for 27% of the time, Pallas kernels for 0%

profile of v1, /device:TPU:13, one launch (start us, length us, event | category | flops | bytes accessed | tf_op | source)
XLA Modules:
  0.0 328.2 jit_solution(7709053384240778906)
XLA Ops:
  11.4 2.7 convert_element_type.84
  17.4 3.7 %reshape.124 = bf16[16,28,2048]{2,1,0:T(8,128)(2,1)} reshape(bf16[448,2048]{1,0:T(8,128)(2,1)} %convolution_convert_fusion.3) | data formatting | bytes 3670016 | tf_op jit(solution)/shard_map/reshape | solution.py:111
  21.1 6.7 %all-to-all-start.2 = ((bf16[16,28,2048]{2,1,0:T(8,128)(2,1)}), bf16[16,28,2048]{2,1,0:T(8,128)(2,1)S(1)}, u32[]{:S(2)}, u32[]{:S(2)}) async-start(bf16[16,28,2048]{2,1,0:T(8,128)(2,1)} %reshape.124), calls=%async_computation.2 | async-start | bytes 4194304 | tf_op jit(solution)/shard_map/all_to_all | solution.py:110
  31.0 3.5 %reshape.119 = bf16[16,28,2048]{2,1,0:T(8,128)(2,1)} reshape(bf16[448,2048]{1,0:T(8,128)(2,1)} %convolution_convert_fusion.4) | data formatting | bytes 3670016 | tf_op jit(solution)/shard_map/reshape | solution.py:65
  34.5 41.1 %all-to-all-done.2 = bf16[16,28,2048]{2,1,0:T(8,128)(2,1)S(1)} async-done(((bf16[16,28,2048]{2,1,0:T(8,128)(2,1)}), bf16[16,28,2048]{2,1,0:T(8,128)(2,1)S(1)}, u32[]{:S(2)}, u32[]{:S(2)}) %all-to-all-start.2) | async-done | bytes 1835040 | tf_op jit(solution)/shard_map/all_to_all | solution.py:110
  75.6 4.4 %all-to-all-start = ((bf16[16,28,2048]{2,1,0:T(8,128)(2,1)}), bf16[16,28,2048]{2,1,0:T(8,128)(2,1)}, u32[]{:S(2)}, u32[]{:S(2)}) async-start(bf16[16,28,2048]{2,1,0:T(8,128)(2,1)} %reshape.119), calls=%async_computation | async-start | bytes 4194304 | tf_op jit(solution)/shard_map/all_to_all | solution.py:66
  82.4 45.4 %all-to-all-done = bf16[16,28,2048]{2,1,0:T(8,128)(2,1)} async-done(((bf16[16,28,2048]{2,1,0:T(8,128)(2,1)}), bf16[16,28,2048]{2,1,0:T(8,128)(2,1)}, u32[]{:S(2)}, u32[]{:S(2)}) %all-to-all-start) | async-done | bytes 1835040 | tf_op jit(solution)/shard_map/all_to_all | solution.py:66
  127.8 3.6 %reshape.120 = bf16[448,2048]{1,0:T(8,128)(2,1)} reshape(bf16[16,28,2048]{2,1,0:T(8,128)(2,1)} %all-to-all-done) | data formatting | bytes 3670016 | tf_op jit(solution)/shard_map/reshape | solution.py:67
  131.4 4.6 %fusion = f32[448,768]{1,0:T(8,128)} fusion(bf16[448,2048]{1,0:T(8,128)(2,1)S(1)} %copy-done.4, bf16[1,2048,768]{2,1,0:T(8,128)(2,1)} %all-gather.11.cloned.1.call-done), kind=kOutput, calls=%fused_computation.7 | convolution fusion | flops 1409286144 | bytes 6356992 | tf_op jit(solution)/shard_map/dot_general | solution.py:122
  136.0 5.1 %fusion.6 = f32[448,768]{1,0:T(8,128)} fusion(bf16[448,2048]{1,0:T(8,128)(2,1)} %reshape.120, bf16[1,2048,768]{2,1,0:T(8,128)(2,1)} %all-gather.9.cloned.1.call-done), kind=kOutput, calls=%fused_computation.13 | convolution fusion | flops 1409286144 | bytes 6356992 | tf_op jit(solution)/shard_map/dot_general | solution.py:74
  141.1 7.3 %all-gather.7.cloned.1.call-done = bf16[1,2048,768]{2,1,0:T(8,128)(2,1)} async-done(((bf16[1,1024,768]{2,1,0:T(8,128)(2,1)}), bf16[1,2048,768]{2,1,0:T(8,128)(2,1)}) %all-gather.7.cloned.1.call-update) | async-done | bytes 3145744 | tf_op jit(solution)/shard_map/all_gather | solution.py:69
  148.4 5.3 %multiply_convert_fusion.2 = (bf16[448,768]{1,0:T(8,128)(2,1)S(1)}, bf16[448,768]{1,0:T(8,128)(2,1)S(1)}, bf16[448,768]{1,0:T(8,128)(2,1)S(1)}) fusion(f32[448,768]{1,0:T(8,128)} %fusion, f32[448,768]{1,0:T(8,128)} %fusion.6, bf16[448,2048]{1,0:T(8,128)(2,1)} %reshape.120, bf16[1,2048,768]{2,1,0:T(8,128)(2,1)} %all-gather.7.cloned.1.call-done), kind=kOutput, calls=%fused_computation.31 | convolution fusion | flops 1414447104 | bytes 9797632 | tf_op jit(solution)/shard_map/dot_general | solution.py:73
  159.5 4.5 %pad_maximum_fusion = bf16[2048,2304]{0,1:T(8,128)(2,1)} fusion(bf16[2048,768]{0,1:T(8,128)(2,1)S(1)} %convolution_convert_fusion, bf16[2048,768]{0,1:T(8,128)(2,1)S(1)} %convolution_convert_fusion.1, bf16[2048,768]{0,1:T(8,128)(2,1)S(1)} %convolution_convert_fusion.2), kind=kLoop, calls=%fused_computation.2 | loop fusion | flops 28311552 | bytes 18874368 | tf_op jit(solution)/shard_map/concatenate | solution.py:149
  164.6 3.7 %fusion.4 = f32[448,2048]{1,0:T(8,128)S(1)} fusion(bf16[448,768]{1,0:T(8,128)(2,1)S(1)} %get-tuple-element.41, bf16[1,2048,768]{2,1,0:T(8,128)(2,1)} %all-gather.9.cloned.1.call-done), kind=kOutput, calls=%fused_computation.11 | convolution fusion | flops 1409286144 | bytes 7503872 | tf_op jit(solution)/shard_map/dot_general | solution.py:26
  168.3 2.9 add_convert_fusion
  180.7 6.5 %all-to-all-start.1 = ((bf16[16,28,2048]{2,1,0:T(8,128)(2,1)}), bf16[16,28,2048]{2,1,0:T(8,128)(2,1)}, u32[]{:S(2)}, u32[]{:S(2)}) async-start(bf16[16,28,2048]{2,1,0:T(8,128)(2,1)} %reshape.121), calls=%async_computation.1 | async-start | bytes 4194304 | tf_op jit(solution)/shard_map/all_to_all | solution.py:79
  191.9 10.5 %collective-permute-done.1 = bf16[1,28,2048]{2,1,0:T(8,128)(2,1)S(1)} collective-permute-done((bf16[1,28,2048]{2,1,0:T(8,128)(2,1)S(1)}, bf16[1,28,2048]{2,1,0:T(8,128)(2,1)S(1)}, u32[]{:S(2)}, u32[]{:S(2)}) %collective-permute-start.1) | collective-permute-done | bytes 114720 | tf_op jit(solution)/shard_map/ppermute | solution.py:20
  202.3 3.9 %collective-permute-start.6 = (bf16[1,28,2048]{2,1,0:T(8,128)(2,1)S(1)}, bf16[1,28,2048]{2,1,0:T(8,128)(2,1)S(1)}, u32[]{:S(2)}, u32[]{:S(2)}) collective-permute-start(bf16[1,28,2048]{2,1,0:T(8,128)(2,1)S(1)} %get-tuple-element.51), channel_id=1, source_target_pairs={{0,7},{1,6},{2,5},{3,4},{4,3},{5,2},{6,1},{7,0},{8,15},{9,14},{10,... | collective-permute-start | bytes 344072 | tf_op jit(solution)/shard_map/ppermute | solution.py:20
  206.9 3.8 %collective-permute-start.7 = (bf16[1,28,2048]{2,1,0:T(8,128)(2,1)S(1)}, bf16[1,28,2048]{2,1,0:T(8,128)(2,1)S(1)}, u32[]{:S(2)}, u32[]{:S(2)}) collective-permute-start(bf16[1,28,2048]{2,1,0:T(8,128)(2,1)S(1)} %get-tuple-element.50), channel_id=1, source_target_pairs={{0,8},{1,9},{2,10},{3,11},{4,12},{5,13},{6,14},{7,15},{8,0},{9,1},... | collective-permute-start | bytes 344072 | tf_op jit(solution)/shard_map/ppermute | solution.py:20
  211.4 14.2 %collective-permute-done.3 = bf16[1,28,2048]{2,1,0:T(8,128)(2,1)S(1)} collective-permute-done((bf16[1,28,2048]{2,1,0:T(8,128)(2,1)S(1)}, bf16[1,28,2048]{2,1,0:T(8,128)(2,1)S(1)}, u32[]{:S(2)}, u32[]{:S(2)}) %collective-permute-start.3) | collective-permute-done | bytes 114720 | tf_op jit(solution)/shard_map/ppermute | solution.py:20
  231.0 3.9 %collective-permute-start.10 = (bf16[1,28,2048]{2,1,0:T(8,128)(2,1)S(1)}, bf16[1,28,2048]{2,1,0:T(8,128)(2,1)S(1)}, u32[]{:S(2)}, u32[]{:S(2)}) collective-permute-start(bf16[1,28,2048]{2,1,0:T(8,128)(2,1)S(1)} %get-tuple-element.47), channel_id=1, source_target_pairs={{0,11},{1,10},{2,9},{3,8},{4,15},{5,14},{6,13},{7,12},{8,3},{9,2},... | collective-permute-start | bytes 344072 | tf_op jit(solution)/shard_map/ppermute | solution.py:20
  237.2 13.2 %collective-permute-done.7 = bf16[1,28,2048]{2,1,0:T(8,128)(2,1)S(1)} collective-permute-done((bf16[1,28,2048]{2,1,0:T(8,128)(2,1)S(1)}, bf16[1,28,2048]{2,1,0:T(8,128)(2,1)S(1)}, u32[]{:S(2)}, u32[]{:S(2)}) %collective-permute-start.7) | collective-permute-done | bytes 114720 | tf_op jit(solution)/shard_map/ppermute | solution.py:20
  255.0 6.7 %collective-permute-done.9 = bf16[1,28,2048]{2,1,0:T(8,128)(2,1)S(1)} collective-permute-done((bf16[1,28,2048]{2,1,0:T(8,128)(2,1)S(1)}, bf16[1,28,2048]{2,1,0:T(8,128)(2,1)S(1)}, u32[]{:S(2)}, u32[]{:S(2)}) %collective-permute-start.9) | collective-permute-done | bytes 114720 | tf_op jit(solution)/shard_map/ppermute | solution.py:20
  265.3 3.8 %collective-permute-done.11 = bf16[1,28,2048]{2,1,0:T(8,128)(2,1)S(1)} collective-permute-done((bf16[1,28,2048]{2,1,0:T(8,128)(2,1)S(1)}, bf16[1,28,2048]{2,1,0:T(8,128)(2,1)S(1)}, u32[]{:S(2)}, u32[]{:S(2)}) %collective-permute-start.11) | collective-permute-done | bytes 114720 | tf_op jit(solution)/shard_map/ppermute | solution.py:20
  269.8 5.7 %collective-permute-done.12 = bf16[1,28,2048]{2,1,0:T(8,128)(2,1)S(1)} collective-permute-done((bf16[1,28,2048]{2,1,0:T(8,128)(2,1)S(1)}, bf16[1,28,2048]{2,1,0:T(8,128)(2,1)S(1)}, u32[]{:S(2)}, u32[]{:S(2)}) %collective-permute-start.12) | collective-permute-done | bytes 114720 | tf_op jit(solution)/shard_map/ppermute | solution.py:20
  290.8 4.2 %multiply_reduce_fusion = (f32[256]{0:T(256)S(1)}, f32[256,2048]{1,0:T(8,128)}, f32[256,2048]{1,0:T(8,128)S(1)}) fusion(f32[256,2048]{1,0:T(8,128)} %copy-done.2, f32[256]{0:T(256)S(1)} %get-tuple-element.63, bf16[256,2048]{1,0:T(8,128)(2,1)} %gather_fusion, pred[256]{0:T(512)(128)(4,1)S(1)} %copy-done.11, f32[256]{0:T(256)S(1)} %mul.91, ...), kind=kLoop, calls=%fused_computation.22 | loop fusion | flops 4718336 | bytes 8391936 | tf_op jit(solution)/shard_map/reduce_sum | solution.py:102
  295.0 3.5 %reshape.123 = f32[128,2,2048]{2,1,0:T(2,128)} reshape(f32[256,2048]{1,0:T(8,128)} %get-tuple-element.60) | data formatting | bytes 4194304 | tf_op jit(solution)/shard_map/reshape | solution.py:98
  300.7 5.1 %reduce_sum.72 = bf16[128,2048]{1,0:T(8,128)(2,1)} reduce(f32[128,2,2048]{2,1,0:T(2,128)} %reshape.123, f32[]{:T(128)} %constant.10.clone.1), dimensions={1}, to_apply=%region_6.8 | reduce | flops 262144 | bytes 2621444 | tf_op jit(solution)/shard_map/reduce_sum | solution.py:99
  305.9 3.8 %reduce_sum.73 = bf16[128,2048]{1,0:T(8,128)(2,1)} reduce(f32[128,2,2048]{2,1,0:T(2,128)S(1)} %copy-done.3, f32[]{:T(128)} %constant.10.clone.1), dimensions={1}, to_apply=%region_7.9 | reduce | flops 262144 | bytes 2621444 | tf_op jit(solution)/shard_map/reduce_sum | solution.py:146
  310.4 4.5 %slice_bitcast_fusion = (bf16[1,1024,768]{1,2,0:T(8,128)(2,1)S(1)}, bf16[1,1024,768]{1,2,0:T(8,128)(2,1)}, bf16[1,1024,768]{1,2,0:T(8,128)(2,1)}) fusion(bf16[1024,2304]{0,1:T(8,128)(2,1)} %reduce-scatter.2.cloned.1.call-done), kind=kLoop, calls=%fused_computation.27 | loop fusion | bytes 9437184 | tf_op jit(solution)/shard_map/broadcast_in_dim | solution.py:163
  314.9 2.6 copy.46
  317.5 2.6 copy.47
  (129 shorter events, 71.3 us)
Async XLA Ops:
  7.2 21.9 %copy-start = (bf16[128,2048]{1,0:T(8,128)(2,1)S(1)}, bf16[128,2048]{1,0:T(8,128)(2,1)}, u32[]{:S(2)}) copy-start(bf16[128,2048]{1,0:T(8,128)(2,1)} %param.10) | copy-start | bytes 1572868
  7.2 124.2 %all-gather.11.cloned.1.call-start = ((), (), s32[]{:S(2)}) async-start(), calls=%async_computation.7 | async-start | bytes 4718592 | tf_op jit(solution)/shard_map/all_gather | solution.py:77
  14.1 7.0 %copy-start.2 = (f32[256,2048]{1,0:T(8,128)}, f32[256,2048]{1,0:T(8,128)S(1)}, u32[]{:S(2)}) copy-start(f32[256,2048]{1,0:T(8,128)S(1)} %convert_element_type.84) | copy-start | bytes 6291460
  21.1 7.9 %copy-start.10 = (s32[128,2]{0,1:T(2,128)S(1)}, s32[128,2]{0,1:T(2,128)}, u32[]{:S(2)}) copy-start(s32[128,2]{0,1:T(2,128)} %param.12) | copy-start | bytes 3076
  21.1 54.5 %all-to-all-start.2 = ((bf16[16,28,2048]{2,1,0:T(8,128)(2,1)}), bf16[16,28,2048]{2,1,0:T(8,128)(2,1)S(1)}, u32[]{:S(2)}, u32[]{:S(2)}) async-start(bf16[16,28,2048]{2,1,0:T(8,128)(2,1)} %reshape.124), calls=%async_computation.2 | async-start | bytes 4194304 | tf_op jit(solution)/shard_map/all_to_all | solution.py:110
  27.8 108.2 %all-gather.9.cloned.1.call-start = ((), (), s32[]{:S(2)}) async-start(), calls=%async_computation.6 | async-start | bytes 4718592 | tf_op jit(solution)/shard_map/all_gather | solution.py:70
  75.6 52.2 %all-to-all-start = ((bf16[16,28,2048]{2,1,0:T(8,128)(2,1)}), bf16[16,28,2048]{2,1,0:T(8,128)(2,1)}, u32[]{:S(2)}, u32[]{:S(2)}) async-start(bf16[16,28,2048]{2,1,0:T(8,128)(2,1)} %reshape.119), calls=%async_computation | async-start | bytes 4194304 | tf_op jit(solution)/shard_map/all_to_all | solution.py:66
  80.0 68.4 %all-gather.7.cloned.1.call-start = ((), (), s32[]{:S(2)}) async-start(), calls=%async_computation.5 | async-start | bytes 4718592 | tf_op jit(solution)/shard_map/all_gather | solution.py:69
  80.7 229.7 %reduce-scatter.2.cloned.1.call-start = ((), (), s32[]{:S(2)}) async-start(), calls=%async_computation.4 | async-start | bytes 14155776 | tf_op jit(solution)/shard_map/reduce_scatter | solution.py:148
  82.4 49.0 %copy-start.4 = (bf16[448,2048]{1,0:T(8,128)(2,1)S(1)}, bf16[448,2048]{1,0:T(8,128)(2,1)}, u32[]{:S(2)}) copy-start(bf16[448,2048]{1,0:T(8,128)(2,1)} %reshape.125) | copy-start | bytes 5505028
  153.7 3.9 %copy-start.18 = (bf16[448,768]{1,0:T(8,128)(2,1)}, bf16[448,768]{1,0:T(8,128)(2,1)S(1)}, u32[]{:S(2)}) copy-start(bf16[448,768]{1,0:T(8,128)(2,1)S(1)} %get-tuple-element.40) | copy-start | bytes 2064388
  176.2 14.6 %collective-permute-start = (bf16[1,28,2048]{2,1,0:T(8,128)(2,1)}, bf16[1,28,2048]{2,1,0:T(8,128)(2,1)S(1)}, u32[]{:S(2)}, u32[]{:S(2)}) collective-permute-start(bf16[1,28,2048]{2,1,0:T(8,128)(2,1)} %get-tuple-element.57), channel_id=1, source_target_pairs={{0,1},{1,0},{2,3},{3,2},{4,5},{5,4},{6,7},{7,6},{8,9},{9,8},{10,11... | collective-permute-start | bytes 344072 | tf_op jit(solution)/shard_map/ppermute | solution.py:20
  180.7 6.5 %copy-start.9 = (bf16[1,28,2048]{2,1,0:T(8,128)(2,1)S(1)}, bf16[1,28,2048]{2,1,0:T(8,128)(2,1)}, u32[]{:S(2)}) copy-start(bf16[1,28,2048]{2,1,0:T(8,128)(2,1)} %get-tuple-element.56) | copy-start | bytes 344068
  180.7 6.9 %copy-start.8 = (bf16[1,28,2048]{2,1,0:T(8,128)(2,1)S(1)}, bf16[1,28,2048]{2,1,0:T(8,128)(2,1)}, u32[]{:S(2)}) copy-start(bf16[1,28,2048]{2,1,0:T(8,128)(2,1)} %get-tuple-element.55) | copy-start | bytes 344068
  180.7 8.6 %copy-start.7 = (bf16[1,28,2048]{2,1,0:T(8,128)(2,1)S(1)}, bf16[1,28,2048]{2,1,0:T(8,128)(2,1)}, u32[]{:S(2)}) copy-start(bf16[1,28,2048]{2,1,0:T(8,128)(2,1)} %get-tuple-element.54) | copy-start | bytes 344068
  180.7 105.3 %all-to-all-start.1 = ((bf16[16,28,2048]{2,1,0:T(8,128)(2,1)}), bf16[16,28,2048]{2,1,0:T(8,128)(2,1)}, u32[]{:S(2)}, u32[]{:S(2)}) async-start(bf16[16,28,2048]{2,1,0:T(8,128)(2,1)} %reshape.121), calls=%async_computation.1 | async-start | bytes 4194304 | tf_op jit(solution)/shard_map/all_to_all | solution.py:79
  187.3 15.0 %collective-permute-start.1 = (bf16[1,28,2048]{2,1,0:T(8,128)(2,1)S(1)}, bf16[1,28,2048]{2,1,0:T(8,128)(2,1)S(1)}, u32[]{:S(2)}, u32[]{:S(2)}) collective-permute-start(bf16[1,28,2048]{2,1,0:T(8,128)(2,1)S(1)} %copy-done.9), channel_id=1, source_target_pairs={{0,2},{1,3},{2,0},{3,1},{4,6},{5,7},{6,4},{7,5},{8,10},{9,11},{10,... | collective-permute-start | bytes 344072 | tf_op jit(solution)/shard_map/ppermute | solution.py:20
  187.6 19.3 %collective-permute-start.2 = (bf16[1,28,2048]{2,1,0:T(8,128)(2,1)S(1)}, bf16[1,28,2048]{2,1,0:T(8,128)(2,1)S(1)}, u32[]{:S(2)}, u32[]{:S(2)}) collective-permute-start(bf16[1,28,2048]{2,1,0:T(8,128)(2,1)S(1)} %copy-done.8), channel_id=1, source_target_pairs={{0,3},{1,2},{2,1},{3,0},{4,7},{5,6},{6,5},{7,4},{8,11},{9,10},{10,... | collective-permute-start | bytes 344072 | tf_op jit(solution)/shard_map/ppermute | solution.py:20
  189.4 36.2 %collective-permute-start.3 = (bf16[1,28,2048]{2,1,0:T(8,128)(2,1)S(1)}, bf16[1,28,2048]{2,1,0:T(8,128)(2,1)S(1)}, u32[]{:S(2)}, u32[]{:S(2)}) collective-permute-start(bf16[1,28,2048]{2,1,0:T(8,128)(2,1)S(1)} %copy-done.7), channel_id=1, source_target_pairs={{0,4},{1,5},{2,6},{3,7},{4,0},{5,1},{6,2},{7,3},{8,12},{9,13},{10,... | collective-permute-start | bytes 344072 | tf_op jit(solution)/shard_map/ppermute | solution.py:20
  189.7 39.8 %collective-permute-start.4 = (bf16[1,28,2048]{2,1,0:T(8,128)(2,1)S(1)}, bf16[1,28,2048]{2,1,0:T(8,128)(2,1)S(1)}, u32[]{:S(2)}, u32[]{:S(2)}) collective-permute-start(bf16[1,28,2048]{2,1,0:T(8,128)(2,1)S(1)} %get-tuple-element.53), channel_id=1, source_target_pairs={{0,5},{1,4},{2,7},{3,6},{4,1},{5,0},{6,3},{7,2},{8,13},{9,12},{10,... | collective-permute-start | bytes 344072 | tf_op jit(solution)/shard_map/ppermute | solution.py:20
  190.9 40.2 %collective-permute-start.5 = (bf16[1,28,2048]{2,1,0:T(8,128)(2,1)S(1)}, bf16[1,28,2048]{2,1,0:T(8,128)(2,1)S(1)}, u32[]{:S(2)}, u32[]{:S(2)}) collective-permute-start(bf16[1,28,2048]{2,1,0:T(8,128)(2,1)S(1)} %get-tuple-element.52), channel_id=1, source_target_pairs={{0,6},{1,7},{2,4},{3,5},{4,2},{5,3},{6,0},{7,1},{8,14},{9,15},{10,... | collective-permute-start | bytes 344072 | tf_op jit(solution)/shard_map/ppermute | solution.py:20
  202.3 33.5 %collective-permute-start.6 = (bf16[1,28,2048]{2,1,0:T(8,128)(2,1)S(1)}, bf16[1,28,2048]{2,1,0:T(8,128)(2,1)S(1)}, u32[]{:S(2)}, u32[]{:S(2)}) collective-permute-start(bf16[1,28,2048]{2,1,0:T(8,128)(2,1)S(1)} %get-tuple-element.51), channel_id=1, source_target_pairs={{0,7},{1,6},{2,5},{3,4},{4,3},{5,2},{6,1},{7,0},{8,15},{9,14},{10,... | collective-permute-start | bytes 344072 | tf_op jit(solution)/shard_map/ppermute | solution.py:20
  206.9 43.5 %collective-permute-start.7 = (bf16[1,28,2048]{2,1,0:T(8,128)(2,1)S(1)}, bf16[1,28,2048]{2,1,0:T(8,128)(2,1)S(1)}, u32[]{:S(2)}, u32[]{:S(2)}) collective-permute-start(bf16[1,28,2048]{2,1,0:T(8,128)(2,1)S(1)} %get-tuple-element.50), channel_id=1, source_target_pairs={{0,8},{1,9},{2,10},{3,11},{4,12},{5,13},{6,14},{7,15},{8,0},{9,1},... | collective-permute-start | bytes 344072 | tf_op jit(solution)/shard_map/ppermute | solution.py:20
  225.5 27.9 %collective-permute-start.8 = (bf16[1,28,2048]{2,1,0:T(8,128)(2,1)S(1)}, bf16[1,28,2048]{2,1,0:T(8,128)(2,1)S(1)}, u32[]{:S(2)}, u32[]{:S(2)}) collective-permute-start(bf16[1,28,2048]{2,1,0:T(8,128)(2,1)S(1)} %get-tuple-element.49), channel_id=1, source_target_pairs={{0,9},{1,8},{2,11},{3,10},{4,13},{5,12},{6,15},{7,14},{8,1},{9,0},... | collective-permute-start | bytes 344072 | tf_op jit(solution)/shard_map/ppermute | solution.py:20
  229.5 32.1 %collective-permute-start.9 = (bf16[1,28,2048]{2,1,0:T(8,128)(2,1)S(1)}, bf16[1,28,2048]{2,1,0:T(8,128)(2,1)S(1)}, u32[]{:S(2)}, u32[]{:S(2)}) collective-permute-start(bf16[1,28,2048]{2,1,0:T(8,128)(2,1)S(1)} %get-tuple-element.48), channel_id=1, source_target_pairs={{0,10},{1,11},{2,8},{3,9},{4,14},{5,15},{6,12},{7,13},{8,2},{9,3},... | collective-permute-start | bytes 344072 | tf_op jit(solution)/shard_map/ppermute | solution.py:20
  231.0 33.6 %collective-permute-start.10 = (bf16[1,28,2048]{2,1,0:T(8,128)(2,1)S(1)}, bf16[1,28,2048]{2,1,0:T(8,128)(2,1)S(1)}, u32[]{:S(2)}, u32[]{:S(2)}) collective-permute-start(bf16[1,28,2048]{2,1,0:T(8,128)(2,1)S(1)} %get-tuple-element.47), channel_id=1, source_target_pairs={{0,11},{1,10},{2,9},{3,8},{4,15},{5,14},{6,13},{7,12},{8,3},{9,2},... | collective-permute-start | bytes 344072 | tf_op jit(solution)/shard_map/ppermute | solution.py:20
  235.8 33.3 %collective-permute-start.11 = (bf16[1,28,2048]{2,1,0:T(8,128)(2,1)S(1)}, bf16[1,28,2048]{2,1,0:T(8,128)(2,1)S(1)}, u32[]{:S(2)}, u32[]{:S(2)}) collective-permute-start(bf16[1,28,2048]{2,1,0:T(8,128)(2,1)S(1)} %get-tuple-element.46), channel_id=1, source_target_pairs={{0,12},{1,13},{2,14},{3,15},{4,8},{5,9},{6,10},{7,11},{8,4},{9,5},... | collective-permute-start | bytes 344072 | tf_op jit(solution)/shard_map/ppermute | solution.py:20
  250.4 25.1 %collective-permute-start.12 = (bf16[1,28,2048]{2,1,0:T(8,128)(2,1)S(1)}, bf16[1,28,2048]{2,1,0:T(8,128)(2,1)S(1)}, u32[]{:S(2)}, u32[]{:S(2)}) collective-permute-start(bf16[1,28,2048]{2,1,0:T(8,128)(2,1)S(1)} %get-tuple-element.45), channel_id=1, source_target_pairs={{0,13},{1,12},{2,15},{3,14},{4,9},{5,8},{6,11},{7,10},{8,5},{9,4},... | collective-permute-start | bytes 344072 | tf_op jit(solution)/shard_map/ppermute | solution.py:20
  253.4 24.1 %collective-permute-start.13 = (bf16[1,28,2048]{2,1,0:T(8,128)(2,1)S(1)}, bf16[1,28,2048]{2,1,0:T(8,128)(2,1)S(1)}, u32[]{:S(2)}, u32[]{:S(2)}) collective-permute-start(bf16[1,28,2048]{2,1,0:T(8,128)(2,1)S(1)} %get-tuple-element.44), channel_id=1, source_target_pairs={{0,14},{1,15},{2,12},{3,13},{4,10},{5,11},{6,8},{7,9},{8,6},{9,7},... | collective-permute-start | bytes 344072 | tf_op jit(solution)/shard_map/ppermute | solution.py:20
  261.6 19.0 %collective-permute-start.14 = (bf16[1,28,2048]{2,1,0:T(8,128)(2,1)S(1)}, bf16[1,28,2048]{2,1,0:T(8,128)(2,1)S(1)}, u32[]{:S(2)}, u32[]{:S(2)}) collective-permute-start(bf16[1,28,2048]{2,1,0:T(8,128)(2,1)S(1)} %get-tuple-element.43), channel_id=1, source_target_pairs={{0,15},{1,14},{2,13},{3,12},{4,11},{5,10},{6,9},{7,8},{8,7},{9,6},... | collective-permute-start | bytes 344072 | tf_op jit(solution)/shard_map/ppermute | solution.py:20
  300.7 5.1 %copy-start.3 = (f32[128,2,2048]{2,1,0:T(2,128)S(1)}, f32[128,2,2048]{2,1,0:T(2,128)}, u32[]{:S(2)}) copy-start(f32[128,2,2048]{2,1,0:T(2,128)} %reshape.128) | copy-start | bytes 6291460
  317.5 4.2 %copy-start.1 = (bf16[128,2048]{1,0:T(8,128)(2,1)S(1)}, bf16[128,2048]{1,0:T(8,128)(2,1)}, u32[]{:S(2)}) copy-start(bf16[128,2048]{1,0:T(8,128)(2,1)} %param.10) | copy-start | bytes 1572868
  (10 other events, 27.2 us)
Sparse Core Ops, SparseCore 0:
  9.5 45.8 all-gather.10
  57.0 44.8 all-gather.8
  103.5 44.8 all-gather.6
  164.1 110.6 reduce-scatter.1
